TPU v7x, 32 devices: a whole 2x2x4 slice. The times are simulated.
32 devices in a mesh: row: 8 (over y, x, core), blk: 4 (over z).
Axes of the slice: x: 2, y: 2, z: 4, core: 2. Of those that a mesh axis runs over, the one named last changes fastest.
Arguments:
- values: bfloat16 [512, 16, 256, 256], P('row', 'blk'), may hold values from -6 to 6
- scales: bfloat16 [512, 16], P('row', 'blk'), may hold values from 0.0049743652 to 0.049804688
- pattern: int32 [512, 16], P('row', 'blk'), may hold values from 0 to 2047, as said below
- omega: bfloat16 [2048, 256, 128], P(('row', 'blk')), may hold values from -6 to 6
Outputs:
- basis: float32 [2048, 256, 128], P(('row', 'blk'))
- upper: float32 [128, 128], replicated
Inputs may be any that keep to these rules, and one draw needn't show every extreme that they name: `pattern`: A block-row of group g = r // 64 has all its column blocks in g * 256 to (g + 1) * 256 - 1. Among the 256 blocks of one device (its block-rows and its positions), at most 64 lie in one aligned run of 64 column blocks, and some run holds exactly 64.
All inputs are finite; a program needn't handle non-finite values.
Results may differ from a plain program's by a relative error of at most 0.0003.
Values may be sent and summed in bfloat16 or wider, within the bound.
A program may use at most 192 MiB of HBM per device.

v0:
```python
import jax
import jax.numpy as jnp
from jax import lax
from jax.sharding import PartitionSpec as P

BS = 256
NCB = 2048


def local(values, scales, pattern, omega):
    rows_dev, per_dev = pattern.shape
    col_dev, block_side, basis_width = omega.shape
    cycle_size = lax.axis_size("blk")
    group_cols = col_dev * cycle_size
    group_base = lax.axis_index("row") * group_cols
    block_count = rows_dev * per_dev
    flat_cols = pattern.reshape(-1) - group_base
    weights = scales.astype(jnp.float32).reshape(rows_dev, per_dev, 1, 1)
    omega_slab = lax.all_gather(omega, "blk", axis=0, tiled=True)
    picked = jnp.take(omega_slab, flat_cols, axis=0)
    picked = picked.reshape(rows_dev, per_dev, block_side, basis_width)
    products = (
        jnp.einsum("rkij,rkjc->rkic", values, picked, preferred_element_type=jnp.float32) * weights
    )
    partial_value = jnp.sum(products, axis=1)
    row_total = lax.psum(partial_value, "blk")
    row_high = lax.optimization_barrier(row_total.astype(jnp.bfloat16))
    row_low = (row_total - row_high.astype(jnp.float32)).astype(jnp.bfloat16)
    high_part = jnp.einsum("rkji,rjc->rkic", values, row_high, preferred_element_type=jnp.float32)
    low_part = jnp.einsum("rkji,rjc->rkic", values, row_low, preferred_element_type=jnp.float32)
    contrib = (high_part + low_part) * weights
    contrib = contrib.reshape(block_count, block_side, basis_width)
    select_map = (flat_cols[None, :] == jnp.arange(col_dev * lax.axis_size("blk"))[:, None]).astype(
        jnp.float32
    )
    column_total = lax.psum_scatter(
        jnp.einsum("cs,sij->cij", select_map, contrib, precision=lax.Precision.HIGHEST),
        "blk",
        scatter_dimension=0,
        tiled=True,
    )
    flat_sum = column_total.reshape(col_dev * block_side, basis_width)
    gram_local = jnp.dot(flat_sum.T, flat_sum, precision=lax.Precision.HIGHEST)
    gram = lax.psum(gram_local, ("row", "blk")) / (NCB * BS)
    lower_factor = jnp.linalg.cholesky(gram)
    solved = jax.scipy.linalg.solve_triangular(lower_factor, flat_sum.T, lower=True)
    return (solved.T.reshape(col_dev, block_side, basis_width), lower_factor.T)


def solution(mesh):
    return jax.shard_map(
        local,
        mesh=mesh,
        in_specs=(
            P("row", "blk", None, None),
            P("row", "blk"),
            P("row", "blk"),
            P(("row", "blk"), None, None),
        ),
        out_specs=(P(("row", "blk"), None, None), P()),
        check_vma=False,
    )
```

profile of v0, /device:TPU:1, one launch (start us, length us, event | category | flops | bytes accessed | tf_op | source)
XLA Modules:
  0.0 1515.9 jit_solution(17570746148987104881)
XLA Ops:
  7.2 0.0 all-gather.2.cloned.1.call-start
  7.2 0.7 all-gather.2.cloned.1.call-update
  7.9 0.0 all-reduce.3.cloned.1.call-start
  7.9 0.7 compare_and_fusion
  8.6 0.1 copy.33
  8.8 0.1 copy.32
  8.9 0.1 sub.32
  9.0 0.8 copy.36
  9.8 288.8 %all-gather.2.cloned.1.call-done = bf16[256,256,128]{2,1,0:T(8,128)(2,1)} async-done(((bf16[64,256,128]{2,1,0:T(8,128)(2,1)}), bf16[256,256,128]{2,1,0:T(8,128)(2,1)}) %all-gather.2.cloned.1.call-update) | async-done | bytes 16777232 | tf_op jit(solution)/shard_map/all_gather | solution.py:19
  298.6 15.5 %gather_fusion = bf16[256,256,128]{2,1,0:T(8,128)(2,1)} fusion(bf16[256,256,128]{2,1,0:T(8,128)(2,1)} %all-gather.2.cloned.1.call-done, s32[1024]{0:T(1024)S(1)} %pad_clamp_fusion), kind=kCustom, calls=%fused_computation | custom fusion | bytes 33555456 | tf_op jit(solution)/shard_map/jit(_take)/gather | solution.py:20
  314.1 22.4 %copy.35 = bf16[64,4,256,128]{2,3,1,0:T(8,128)(2,1)} copy(bf16[64,4,256,128]{3,2,1,0:T(8,128)(2,1)} %bitcast.41) | data formatting | bytes 33554432 | tf_op jit(solution)/shard_map/jit(_take)/gather | solution.py:20
  336.5 22.9 %multiply_reduce_fusion = f32[64,128,256]{2,1,0:T(8,128)} fusion(f32[64,4]{1,0:T(8,128)S(1)} %copy.36, bf16[64,4,256,256]{3,2,1,0:T(8,128)(2,1)} %param.4, bf16[64,4,256,128]{2,3,1,0:T(8,128)(2,1)} %copy.35, pred[64,4]{1,0:T(8,128)(4,1)S(1)} %copy.33), kind=kOutput, calls=%fused_computation.2 | convolution fusion | flops 4318035968 | bytes 58721536 | tf_op jit(solution)/shard_map/rkij,rkjc->rkic/dot_general | solution.py:23
  359.4 0.0 all-reduce.3.cloned.1.call-update
  359.5 0.2 reduce-scatter.2.cloned.1.call-start
  359.7 0.1 sub.31
  359.8 288.5 %all-reduce.3.cloned.1.call-done = f32[64,256,128]{1,2,0:T(8,128)} async-done(((f32[64,256,128]{1,2,0:T(8,128)}), f32[64,256,128]{1,2,0:T(8,128)}) %all-reduce.3.cloned.1.call-update) | async-done | bytes 8388624 | tf_op jit(solution)/shard_map/psum | solution.py:26
  648.3 4.0 convert_element_type.14
  652.3 0.0 copy-start
  652.3 2.0 copy-done
  654.3 24.7 %fusion.10 = f32[64,128,4,256]{3,1,2,0:T(8,128)} fusion(bf16[64,4,256,256]{3,2,1,0:T(8,128)(2,1)} %param.4, bf16[64,256,128]{1,2,0:T(8,128)(2,1)S(1)} %convert_element_type.14), kind=kOutput, calls=%fused_computation.11 | convolution fusion | flops 4294967296 | bytes 71303168 | tf_op jit(solution)/shard_map/rkji,rjc->rkic/dot_general | solution.py:29
  679.0 38.1 %add_multiply_fusion = f32[64,128,4,256]{3,1,2,0:T(8,128)} fusion(f32[64,128,4,256]{3,1,2,0:T(8,128)} %fusion.10, f32[64,4]{1,0:T(8,128)S(1)} %copy.36, bf16[64,4,256,256]{3,2,1,0:T(8,128)(2,1)} %param.4, f32[64,256,128]{1,2,0:T(8,128)} %all-reduce.3.cloned.1.call-done, bf16[64,256,128]{1,2,0:T(8,128)(2,1)} %copy-done), kind=kOutput, calls=%fused_computation.1 | convolution fusion | flops 4318035968 | bytes 113247232 | tf_op jit(solution)/shard_map/rkji,rjc->rkic/dot_general | solution.py:30
  717.1 31.1 %copy.38 = f32[256,256,128]{2,0,1:T(8,128)} copy(f32[256,256,128]{1,2,0:T(8,128)} %bitcast.40) | data formatting | bytes 67108864 | tf_op jit(solution)/shard_map/reshape | solution.py:32
  748.2 28.9 %fusion.13 = f32[256,256,128]{2,0,1:T(8,128)} fusion(f32[256,256,128]{2,0,1:T(8,128)} %copy.38, s32[256]{0:T(256)S(1)} %sub.31), kind=kOutput, calls=%fused_computation.16 | convolution fusion | flops 25769869312 | bytes 67109888 | tf_op jit(solution)/shard_map/cs,sij->cij/dot_general | solution.py:37
  777.1 0.0 reduce-scatter.2.cloned.1.call-update
  777.1 0.3 all-reduce.5.cloned.1.call-start
  777.3 550.8 %reduce-scatter.2.cloned.1.call-done = f32[64,256,128]{2,0,1:T(8,128)} async-done(((f32[256,256,128]{2,0,1:T(8,128)}), f32[64,256,128]{2,0,1:T(8,128)}) %reduce-scatter.2.cloned.1.call-update) | async-done | bytes 8388624 | tf_op jit(solution)/shard_map/reduce_scatter | solution.py:36
  1328.2 17.6 %convolution_bitcast_fusion = f32[128,128]{0,1:T(8,128)} fusion(f32[64,256,128]{2,0,1:T(8,128)} %reduce-scatter.2.cloned.1.call-done), kind=kOutput, calls=%fused_computation.13 | convolution fusion | flops 3221225472 | bytes 8454144 | tf_op jit(solution)/shard_map/dot_general | solution.py:43
  1345.8 0.0 all-reduce.5.cloned.1.call-update
  1345.8 122.4 %all-reduce.5.cloned.1.call-done = f32[128,128]{0,1:T(8,128)} async-done(((f32[128,128]{0,1:T(8,128)}), f32[128,128]{0,1:T(8,128)}) %all-reduce.5.cloned.1.call-update) | async-done | bytes 65552 | tf_op jit(solution)/shard_map/psum | solution.py:44
  1468.2 0.8 broadcast_multiply_fusion
  1469.0 0.1 copy.40
  1469.1 0.9 fusion.17
  1470.0 11.7 cholesky.16
  1481.7 0.6 compare_reduce_fusion
  1482.4 0.7 fusion.18
  1483.0 0.7 copy.43
  1483.8 9.8 custom-call.7
  1493.6 15.7 %fusion.3 = f32[64,256,128]{2,1,0:T(8,128)} fusion(f32[64,256,128]{2,0,1:T(8,128)} %reduce-scatter.2.cloned.1.call-done, f32[1,128,128]{1,2,0:T(8,128)S(1)} %custom-call.7), kind=kOutput, calls=%fused_computation.6 | convolution fusion | flops 3221225472 | bytes 16842752 | tf_op jit(solution)/shard_map/jit(_solve_triangular)/triangular_solve | solution.py:46
  (3 shorter events, 0.0 us)
Async XLA Ops:
  7.2 291.4 %all-gather.2.cloned.1.call-start = ((), (), s32[]{:S(2)}) async-start(), calls=%async_computation.1 | async-start | bytes 20971520 | tf_op jit(solution)/shard_map/all_gather | solution.py:19
  7.9 640.4 %all-reduce.3.cloned.1.call-start = ((), (), s32[]{:S(2)}) async-start(), calls=%async_computation.2 | async-start | bytes 16777216 | tf_op jit(solution)/shard_map/psum | solution.py:26
  359.5 968.7 %reduce-scatter.2.cloned.1.call-start = ((), (), s32[]{:S(2)}) async-start(), calls=%async_computation.3 | async-start | bytes 41943040 | tf_op jit(solution)/shard_map/reduce_scatter | solution.py:36
  652.3 2.0 copy-start
  777.1 691.1 %all-reduce.5.cloned.1.call-start = ((), (), s32[]{:S(2)}) async-start(), calls=%async_computation.4 | async-start | bytes 131072 | tf_op jit(solution)/shard_map/psum | solution.py:44
Sparse Core Ops, SparseCore 0:
  9.5 288.9 all-gather.1
  359.6 288.6 all-reduce.2
  777.2 550.9 reduce-scatter.1
  1345.9 122.2 all-reduce.4
where the time goes:
time: 1520 us
  waiting for transfers between devices  1250 us (82%)
  matrix products  148 us (10%)
  local copies, waits for them, and re-layouts  73.1 us (5%)
  other arithmetic  29.2 us (2%)
    reduce_scatter x1, waiting for transfers between devices, local(): lax.psum_scatter(jnp.einsum('cs,sij->cij', select_map, contrib, precision...  551 us
    all_gather x1, waiting for transfers between devices, local(): omega_slab = lax.all_gather(omega, 'blk', axis=0, tiled=True)  289 us
    psum x1, waiting for transfers between devices, local(): row_total = lax.psum(partial_value, 'blk')  289 us
    psum x1, waiting for transfers between devices, local(): gram = lax.psum(gram_local, ('row', 'blk')) / (NCB * BS)  122 us
    dot_general x1, matrix products, local(): jnp.einsum('rkji,rjc->rkic', values, row_low, preferred_element_type=jnp....  38.1 us
    gather x2, local copies, waits for them, and re-layouts, local(): picked = jnp.take(omega_slab, flat_cols, axis=0)  37.9 us
    reshape x1, local copies, waits for them, and re-layouts, local(): contrib = contrib.reshape(block_count, block_side, basis_width)  31.1 us
  transfers between devices with their start and end apart: 4, of which 4 were waited for; matrix products, arithmetic and copies ran while one was open for 0% of the time, Pallas kernels for 0%

commit v1 on v0

--- a/solution.py
+++ b/solution.py
@@ -23,7 +23,8 @@
         jnp.einsum("rkij,rkjc->rkic", values, picked, preferred_element_type=jnp.float32) * weights
     )
     partial_value = jnp.sum(products, axis=1)
-    row_total = lax.psum(partial_value, "blk")
+    parts = lax.all_gather(partial_value, "blk")
+    row_total = jnp.sum(parts, axis=0)
     row_high = lax.optimization_barrier(row_total.astype(jnp.bfloat16))
     row_low = (row_total - row_high.astype(jnp.float32)).astype(jnp.bfloat16)
     high_part = jnp.einsum("rkji,rjc->rkic", values, row_high, preferred_element_type=jnp.float32)

time: 1520 us -> 1810 us (1.19)
  waiting for transfers between devices: 1250 us -> 1520 us
    all_gather x0 -> x1, waiting for transfers between devices: none -> 559 us  [local(): parts = lax.all_gather(partial_value, 'blk')]
    psum x1 -> x0, waiting for transfers between devices: 289 us -> none  [local(): row_total = lax.psum(partial_value, 'blk')]
where the time goes in v1:
time: 1810 us
  waiting for transfers between devices  1520 us (84%)
  matrix products  146 us (8%)
  local copies, waits for them, and re-layouts  80 us (4%)
  other arithmetic  47.2 us (3%)
    all_gather x1, waiting for transfers between devices, local(): parts = lax.all_gather(partial_value, 'blk')  559 us
    reduce_scatter x1, waiting for transfers between devices, local(): lax.psum_scatter(jnp.einsum('cs,sij->cij', select_map, contrib, precision...  550 us
    all_gather x1, waiting for transfers between devices, local(): omega_slab = lax.all_gather(omega, 'blk', axis=0, tiled=True)  289 us
    psum x1, waiting for transfers between devices, local(): gram = lax.psum(gram_local, ('row', 'blk')) / (NCB * BS)  122 us
    dot_general x1, matrix products, local(): jnp.einsum('rkji,rjc->rkic', values, row_low, preferred_element_type=jnp....  38.2 us
    gather x2, local copies, waits for them, and re-layouts, local(): picked = jnp.take(omega_slab, flat_cols, axis=0)  37.9 us
  transfers between devices with their start and end apart: 4, of which 4 were waited for; matrix products, arithmetic and copies ran while one was open for 0% of the time, Pallas kernels for 0%

profile of v1, /device:TPU:1, one launch (start us, length us, event | category | flops | bytes accessed | tf_op | source)
XLA Modules:
  0.0 1808.9 jit_solution(18278649318235528508)
XLA Ops:
  7.2 0.0 all-gather.4.cloned.1.call-start
  7.2 0.7 all-gather.4.cloned.1.call-update
  7.9 0.0 all-gather.6.cloned.1.call-start
  7.9 0.7 compare_and_fusion
  8.6 0.1 copy.45
  8.8 0.1 copy.44
  8.9 0.1 sub.32
  9.0 0.8 copy.48
  9.8 288.8 %all-gather.4.cloned.1.call-done = bf16[256,256,128]{2,1,0:T(8,128)(2,1)} async-done(((bf16[64,256,128]{2,1,0:T(8,128)(2,1)}), bf16[256,256,128]{2,1,0:T(8,128)(2,1)}) %all-gather.4.cloned.1.call-update) | async-done | bytes 16777232 | tf_op jit(solution)/shard_map/all_gather | solution.py:19
  298.6 15.5 gather_fusion
  314.1 22.4 %copy.47 = bf16[64,4,256,128]{2,3,1,0:T(8,128)(2,1)} copy(bf16[64,4,256,128]{3,2,1,0:T(8,128)(2,1)} %bitcast.42) | data formatting | bytes 33554432 | tf_op jit(solution)/shard_map/jit(_take)/gather | solution.py:20
  336.5 22.9 %multiply_reduce_fusion = f32[64,128,256]{2,1,0:T(8,128)} fusion(f32[64,4]{1,0:T(8,128)S(1)} %copy.48, bf16[64,4,256,256]{3,2,1,0:T(8,128)(2,1)} %param.4, bf16[64,4,256,128]{2,3,1,0:T(8,128)(2,1)} %copy.47, pred[64,4]{1,0:T(8,128)(4,1)S(1)} %copy.45), kind=kOutput, calls=%fused_computation.2 | convolution fusion | flops 4318035968 | bytes 58721536 | tf_op jit(solution)/shard_map/rkij,rkjc->rkic/dot_general | solution.py:23
  359.4 9.0 copy.49
  368.4 0.0 all-gather.6.cloned.1.call-update
  368.4 0.2 reduce-scatter.2.cloned.1.call-start
  368.7 0.1 sub.31
  368.8 559.4 %all-gather.6.cloned.1.call-done = f32[256,256,128]{2,1,0:T(8,128)} async-done(((f32[64,256,128]{2,1,0:T(8,128)}), f32[256,256,128]{2,1,0:T(8,128)}) %all-gather.6.cloned.1.call-update) | async-done | bytes 33554448 | tf_op jit(solution)/shard_map/all_gather | solution.py:26
  928.2 15.9 reduce_sum.22
  944.0 6.0 convert_element_type.14
  950.1 22.9 %fusion.10 = f32[64,128,4,256]{3,1,2,0:T(8,128)} fusion(bf16[64,4,256,256]{3,2,1,0:T(8,128)(2,1)} %param.4, bf16[64,256,128]{2,1,0:T(8,128)(2,1)} %convert_element_type.14), kind=kOutput, calls=%fused_computation.11 | convolution fusion | flops 4294967296 | bytes 71303168 | tf_op jit(solution)/shard_map/rkji,rjc->rkic/dot_general | solution.py:30
  973.0 38.2 %add_multiply_fusion = f32[64,128,4,256]{3,1,2,0:T(8,128)} fusion(f32[64,128,4,256]{3,1,2,0:T(8,128)} %fusion.10, f32[64,4]{1,0:T(8,128)S(1)} %copy.48, bf16[64,4,256,256]{3,2,1,0:T(8,128)(2,1)} %param.4, f32[64,256,128]{2,1,0:T(8,128)} %reduce_sum.22, bf16[64,256,128]{2,1,0:T(8,128)(2,1)} %convert_element_type.14), kind=kOutput, calls=%fused_computation.1 | convolution fusion | flops 4318035968 | bytes 113247232 | tf_op jit(solution)/shard_map/rkji,rjc->rkic/dot_general | solution.py:31
  1011.2 31.1 %copy.53 = f32[256,256,128]{2,0,1:T(8,128)} copy(f32[256,256,128]{1,2,0:T(8,128)} %bitcast.41) | data formatting | bytes 67108864 | tf_op jit(solution)/shard_map/reshape | solution.py:33
  1042.3 28.9 %fusion.13 = f32[256,256,128]{2,0,1:T(8,128)} fusion(f32[256,256,128]{2,0,1:T(8,128)} %copy.53, s32[256]{0:T(256)S(1)} %sub.31), kind=kOutput, calls=%fused_computation.16 | convolution fusion | flops 25769869312 | bytes 67109888 | tf_op jit(solution)/shard_map/cs,sij->cij/dot_general | solution.py:38
  1071.2 0.0 reduce-scatter.2.cloned.1.call-update
  1071.2 0.3 all-reduce.2.cloned.1.call-start
  1071.4 549.7 %reduce-scatter.2.cloned.1.call-done = f32[64,256,128]{2,0,1:T(8,128)} async-done(((f32[256,256,128]{2,0,1:T(8,128)}), f32[64,256,128]{2,0,1:T(8,128)}) %reduce-scatter.2.cloned.1.call-update) | async-done | bytes 8388624 | tf_op jit(solution)/shard_map/reduce_scatter | solution.py:37
  1621.2 17.6 convolution_bitcast_fusion
  1638.8 0.0 all-reduce.2.cloned.1.call-update
  1638.8 122.4 %all-reduce.2.cloned.1.call-done = f32[128,128]{0,1:T(8,128)} async-done(((f32[128,128]{0,1:T(8,128)}), f32[128,128]{0,1:T(8,128)}) %all-reduce.2.cloned.1.call-update) | async-done | bytes 65552 | tf_op jit(solution)/shard_map/psum | solution.py:45
  1761.2 0.8 broadcast_multiply_fusion
  1762.1 0.1 copy.55
  1762.2 0.9 fusion.17
  1763.0 11.7 cholesky.16
  1774.8 0.6 compare_reduce_fusion
  1775.4 0.7 fusion.18
  1776.1 0.7 copy.58
  1776.8 9.8 custom-call.7
  1786.6 15.7 fusion.3
  (3 shorter events, 0.0 us)
Async XLA Ops:
  7.2 291.4 %all-gather.4.cloned.1.call-start = ((), (), s32[]{:S(2)}) async-start(), calls=%async_computation.1 | async-start | bytes 20971520 | tf_op jit(solution)/shard_map/all_gather | solution.py:19
  7.9 920.3 %all-gather.6.cloned.1.call-start = ((), (), s32[]{:S(2)}) async-start(), calls=%async_computation.4 | async-start | bytes 41943040 | tf_op jit(solution)/shard_map/all_gather | solution.py:26
  368.4 1252.7 %reduce-scatter.2.cloned.1.call-start = ((), (), s32[]{:S(2)}) async-start(), calls=%async_computation.2 | async-start | bytes 41943040 | tf_op jit(solution)/shard_map/reduce_scatter | solution.py:37
  1071.2 690.1 %all-reduce.2.cloned.1.call-start = ((), (), s32[]{:S(2)}) async-start(), calls=%async_computation.3 | async-start | bytes 131072 | tf_op jit(solution)/shard_map/psum | solution.py:45
Sparse Core Ops, SparseCore 0:
  9.5 288.9 all-gather.3
  368.5 559.5 all-gather.5
  1071.3 549.8 reduce-scatter.1
  1638.9 122.2 all-reduce.1
